TPU v7x, 512 devices: a whole 4x8x8 slice. The times are simulated.
512 devices in a mesh: gx: 32 (over y_hi, z, core), gy: 16 (over y_lo, x).
Axes of the slice: x: 4, y: 8 (y_hi: 2, y_lo: 4; y = y_hi * 4 + y_lo), z: 8, core: 2. Of those that a mesh axis runs over, the one named last changes fastest.
Arguments:
- feature: bfloat16 [6, 64, 768, 2048], P(None, None, 'gx', 'gy'), may hold values from -6 to 6
- widths: int32 [32], replicated, may hold values from 8 to 24, as said below
- dw_weight: float32 [27, 64], replicated, may hold values from -1.25 to 1.25
- dw_bias: float32 [64], replicated, may hold values from -3 to 3
- pw_weight: bfloat16 [64, 64], replicated, may hold values from -0.75 to 0.75
- pw_bias: float32 [64], replicated, may hold values from -3 to 3
- lift_weight: float32 [64, 3], replicated, may hold values from -3 to 3
- coarse: float32 [3, 32, 128], P(None, 'gy'), may hold values from -6 to 6
Outputs:
- block_out: bfloat16 [2, 64, 768, 2048], P(None, None, 'gx', 'gy')
Inputs may be any that keep to these rules, and one draw needn't show every extreme that they name: The widths sum to 512; some slab has width exactly 24 and some exactly 8.
All inputs are finite; a program needn't handle non-finite values.
Results may differ from a plain program's by a relative error of at most 0.0031.
Values may be sent and summed in bfloat16 or wider, within the bound.
A program may use at most 64 MiB of HBM per device.

v0:
```python
import jax
import jax.numpy as jnp
from jax import lax
from jax.sharding import PartitionSpec as P

XW = 16
ZOUT = 2
CF = 16


def with_halo(cells, sides, width):
    for axis, dim in sides:
        count = lax.axis_size(axis)
        head = lax.slice_in_dim(cells, 0, width, axis=dim)
        tail = lax.slice_in_dim(cells, cells.shape[dim] - width, cells.shape[dim], axis=dim)
        cells = jnp.concatenate(
            [
                lax.ppermute(tail, axis, [(i, (i + 1) % count) for i in range(count)]),
                cells,
                lax.ppermute(head, axis, [((i + 1) % count, i) for i in range(count)]),
            ],
            axis=dim,
        )
    return cells


def passed_along(shard, axis, by):
    length = lax.axis_size(axis)
    return lax.ppermute(shard, axis, [(i, (i + by) % length) for i in range(length)])


def attach_rows(block, width, from_lower, from_upper):
    rim_shape = list(block.shape)
    rim_shape[2] = 2
    joined = jnp.concatenate([from_lower, block, jnp.zeros(rim_shape, block.dtype)], axis=2)
    return lax.dynamic_update_slice_in_dim(joined, from_upper, width + 2, axis=2)


def shards(feature, widths, dw_weight, dw_bias, pw_weight, pw_bias, lift_weight, coarse):
    slab_index = lax.axis_index("gx")
    width = widths[slab_index]
    starts = jnp.cumsum(widths) - widths
    start = starts[slab_index]
    slots = feature.shape[2]
    tile = feature.shape[3]
    total = XW * lax.axis_size("gx")
    widened = with_halo(feature, (("gy", 3),), 2)
    last_two = lax.dynamic_slice_in_dim(widened, width - 2, 2, axis=2)
    from_lower = passed_along(last_two, "gx", 1)
    from_upper = passed_along(widened[:, :, :2, :], "gx", -1)
    padded = attach_rows(widened, width, from_lower, from_upper)
    depth = (
        jnp.zeros((ZOUT, feature.shape[1], slots, tile), jnp.float32) + dw_bias[None, :, None, None]
    )
    for dz in (-1, 0, 1):
        for dx in (-1, 0, 1):
            for dy in (-1, 0, 1):
                tap = 9 * (dz + 1) + 3 * (dx + 1) + (dy + 1)
                window = padded[
                    2 + 2 * dz : 2 + 2 * dz + ZOUT,
                    :,
                    2 + 2 * dx : 2 + 2 * dx + slots,
                    2 + 2 * dy : 2 + 2 * dy + tile,
                ]
                depth = depth + dw_weight[tap][None, :, None, None] * window.astype(jnp.float32)
    depth = depth.astype(jnp.bfloat16)
    mixed = jnp.einsum("oc,zcxy->zoxy", pw_weight, depth, preferred_element_type=jnp.float32)
    mixed = mixed + pw_bias[None, :, None, None]
    active = jnp.where(mixed > 0, mixed, 0.2 * mixed)
    local = lax.all_to_all(coarse, "gy", split_axis=2, concat_axis=1, tiled=True)
    rows = start + jnp.arange(slots, dtype=jnp.int32)
    cells = rows % total // CF
    onehot = (cells[:, None] == jnp.arange(local.shape[1], dtype=jnp.int32)[None, :]).astype(
        jnp.float32
    )
    along_x = jnp.einsum("xn,knv->kxv", onehot, local, precision=lax.Precision.HIGHEST)
    upsampled = jnp.repeat(along_x, CF, axis=2)
    lifted = jnp.einsum("ck,kxy->cxy", lift_weight, upsampled, precision=lax.Precision.HIGHEST)
    value = feature[2 : 2 + ZOUT].astype(jnp.float32) + active + lifted[None]
    valid = jnp.arange(slots, dtype=jnp.int32) < width
    return jnp.where(valid[None, None, :, None], value, 0.0).astype(jnp.bfloat16)


def solution(mesh):
    placed = (P(None, None, "gx", "gy"), P(), P(), P(), P(), P(), P(), P(None, "gy", None))
    return jax.shard_map(
        shards, mesh=mesh, in_specs=placed, out_specs=P(None, None, "gx", "gy"), check_vma=False
    )
```

profile of v0, /device:TPU:14, one launch (start us, length us, event | category | flops | bytes accessed | tf_op | source)
XLA Modules:
  0.0 79.4 jit_solution(256734089757747484)
XLA Ops:
  0.0 0.0 copy-start
  0.0 4.9 %fusion.11 = (bf16[6,64,24,2]{3,2,1,0:T(8,128)(2,1)S(1)}, bf16[6,64,24,2]{3,2,1,0:T(8,128)(2,1)}) fusion(bf16[6,64,24,128]{3,2,1,0:T(8,128)(2,1)} %param.8), kind=kLoop, calls=%fused_computation.55 | loop fusion | bytes 147456 | tf_op jit(solution)/shard_map/slice | solution.py:15
  4.9 1.4 %copy.53 = bf16[6,64,24,2]{1,2,3,0:T(8,128)(2,1)S(1)} copy(bf16[6,64,24,2]{3,2,1,0:T(8,128)(2,1)S(1)} %get-tuple-element.7) | data formatting | bytes 73728
  6.3 0.0 copy-start.6
  6.3 0.0 copy-start.5
  6.3 0.0 copy-start.8
  6.3 0.0 copy-start.1
  6.4 3.5 %collective-permute-start = (bf16[6,64,24,2]{1,2,3,0:T(8,128)(2,1)S(1)}, bf16[6,64,24,2]{1,2,3,0:T(8,128)(2,1)S(1)}, u32[]{:S(2)}, u32[]{:S(2)}) collective-permute-start(bf16[6,64,24,2]{1,2,3,0:T(8,128)(2,1)S(1)} %copy.53), channel_id=1, source_target_pairs={{0,1},{1,2},{2,3},{3,4},{4,5},{5,6},{6,7},{7,8},{8,9},{9,10},{10,1... | collective-permute-start | bytes 110600 | tf_op jit(solution)/shard_map/ppermute | solution.py:18
  9.9 2.9 %copy.54 = bf16[6,64,24,2]{1,2,3,0:T(8,128)(2,1)S(1)} copy(bf16[6,64,24,2]{3,2,1,0:T(8,128)(2,1)} %get-tuple-element.8) | data formatting | bytes 73728
  12.8 2.4 %collective-permute-start.1 = (bf16[6,64,24,2]{1,2,3,0:T(8,128)(2,1)S(1)}, bf16[6,64,24,2]{1,2,3,0:T(8,128)(2,1)S(1)}, u32[]{:S(2)}, u32[]{:S(2)}) collective-permute-start(bf16[6,64,24,2]{1,2,3,0:T(8,128)(2,1)S(1)} %copy.54), channel_id=1, source_target_pairs={{1,0},{2,1},{3,2},{4,3},{5,4},{6,5},{7,6},{8,7},{9,8},{10,9},{11,1... | collective-permute-start | bytes 110600 | tf_op jit(solution)/shard_map/ppermute | solution.py:20
  15.2 0.0 copy-done.6
  15.2 0.8 %copy.44 = f32[3,2,128]{0,1,2:T(2,128)} copy(f32[3,2,128]{2,1,0:T(2,128)S(1)} %copy-done.6) | data formatting | bytes 6144 | tf_op args[7]
  16.1 13.0 %all-to-all-start = ((f32[3,2,128]{0,1,2:T(2,128)}), f32[3,2,128]{0,1,2:T(2,128)S(1)}, u32[]{:S(2)}, u32[]{:S(2)}) async-start(f32[3,2,128]{0,1,2:T(2,128)} %copy.44), calls=%async_computation | async-start | bytes 262144 | tf_op jit(solution)/shard_map/all_to_all | solution.py:70
  29.0 0.0 copy-done.5
  29.1 0.0 copy-done.8
  29.1 0.6 dynamic_slice.9
  29.7 0.6 iota_compare_fusion.2
  30.3 0.1 copy.43
  30.4 0.1 reduce-window.9
  30.4 0.1 reduce
  30.6 0.7 dynamic_slice.11
  31.2 0.6 and_select_fusion
  31.8 0.0 copy-done.1
  31.9 2.1 %copy.37 = bf16[6,64,24,128]{3,1,2,0:T(8,128)(2,1)} copy(bf16[6,64,24,128]{3,2,1,0:T(8,128)(2,1)S(1)} %copy-done.1) | data formatting | bytes 4718592 | tf_op args[0]
  36.4 0.1 pad.4.clone
  36.5 0.0 all-to-all-done
  36.5 0.3 copy.52
  36.8 0.1 copy.47
  36.9 0.2 convolution_bitcast_fusion.1
  37.1 0.1 copy.48
  37.2 0.1 broadcast_in_dim.24
  37.3 0.1 reshape.95
  37.5 0.0 collective-permute-done
  37.5 2.1 %copy.40 = bf16[6,64,24,2]{3,1,2,0:T(8,128)(2,1)} copy(bf16[6,64,24,2]{1,2,3,0:T(8,128)(2,1)S(1)} %collective-permute-done) | data formatting | bytes 73728 | tf_op jit(solution)/shard_map/ppermute | solution.py:18
  39.6 0.0 copy-start.2
  39.6 0.0 collective-permute-done.1
  39.6 2.1 %copy.42 = bf16[6,64,24,2]{3,1,2,0:T(8,128)(2,1)} copy(bf16[6,64,24,2]{1,2,3,0:T(8,128)(2,1)S(1)} %collective-permute-done.1) | data formatting | bytes 73728 | tf_op jit(solution)/shard_map/ppermute | solution.py:20
  41.7 0.0 copy-done.2
  41.7 0.0 copy-start.7
  41.7 0.0 copy-start.4
  41.7 4.8 %pad_maximum_fusion = bf16[6,64,24,132]{3,1,2,0:T(8,128)(2,1)S(1)} fusion(bf16[6,64,24,2]{3,1,2,0:T(8,128)(2,1)} %copy.42, bf16[6,64,24,128]{3,1,2,0:T(8,128)(2,1)S(1)} %copy-done.2, bf16[6,64,24,2]{3,1,2,0:T(8,128)(2,1)} %copy.40), kind=kLoop, calls=%fused_computation.1 | loop fusion | flops 7299072 | bytes 4866048 | tf_op jit(solution)/shard_map/concatenate | solution.py:16
  46.5 0.0 copy-start.3
  46.6 0.1 fusion.10
  46.6 2.1 %collective-permute-start.2 = (bf16[6,64,2,132]{3,1,2,0:T(8,128)(2,1)S(1)}, bf16[6,64,2,132]{3,1,2,0:T(8,128)(2,1)S(1)}, u32[]{:S(2)}, u32[]{:S(2)}) collective-permute-start(bf16[6,64,2,132]{3,1,2,0:T(8,128)(2,1)S(1)} %get-tuple-element.6), channel_id=1, source_target_pairs={{0,16},{16,32},{32,48},{48,64},{64,80},{80,96},{96,112},{112,128},... | collective-permute-start | bytes 608264 | tf_op jit(solution)/shard_map/ppermute | solution.py:29
  48.7 0.0 copy-done.7
  48.7 0.8 %convolution_bitcast_fusion = f32[64,24,128]{2,0,1:T(8,128)S(1)} fusion(f32[3,24,128]{2,1,0:T(8,128)S(1)} %reshape.95, f32[64,3]{0,1:T(4,128)S(1)} %copy-done.7), kind=kOutput, calls=%fused_computation.8 | convolution fusion | flops 7077888 | bytes 824064 | tf_op jit(solution)/shard_map/ck,kxy->cxy/dot_general | solution.py:78
  49.5 0.0 copy-start.9
  49.5 0.0 copy-start.10
  49.5 9.8 %collective-permute-start.3 = (bf16[6,64,2,132]{3,1,2,0:T(8,128)(2,1)S(1)}, bf16[6,64,2,132]{3,1,2,0:T(8,128)(2,1)S(1)}, u32[]{:S(2)}, u32[]{:S(2)}) collective-permute-start(bf16[6,64,2,132]{3,1,2,0:T(8,128)(2,1)S(1)} %get-tuple-element.5), channel_id=1, source_target_pairs={{0,496},{16,0},{32,16},{48,32},{64,48},{80,64},{96,80},{112,96},{1... | collective-permute-start | bytes 608264 | tf_op jit(solution)/shard_map/ppermute | solution.py:29
  59.4 6.7 %collective-permute-done.2 = bf16[6,64,2,132]{3,1,2,0:T(8,128)(2,1)S(1)} collective-permute-done((bf16[6,64,2,132]{3,1,2,0:T(8,128)(2,1)S(1)}, bf16[6,64,2,132]{3,1,2,0:T(8,128)(2,1)S(1)}, u32[]{:S(2)}, u32[]{:S(2)}) %collective-permute-start.2) | collective-permute-done | bytes 202784 | tf_op jit(solution)/shard_map/ppermute | solution.py:29
  66.1 0.0 copy-done.4
  66.1 0.0 copy-done.3
  66.1 4.1 %maximum_maximum_fusion = bf16[6,64,28,132]{3,1,2,0:T(8,128)(2,1)S(1)} fusion(bf16[6,64,24,2]{3,1,2,0:T(8,128)(2,1)S(1)} %copy-done.4, bf16[6,64,24,128]{3,1,2,0:T(8,128)(2,1)S(1)} %copy-done.2, bf16[6,64,24,2]{3,1,2,0:T(8,128)(2,1)S(1)} %copy-done.3, bf16[6,64,2,132]{3,1,2,0:T(8,128)(2,1)S(1)} %collective-permute-done.2, bf16[28]{0:T(256)(128)(2,1)S(1)} %pad.4.clone), kind=kLoop, calls=%fused_computation | loop fusion | flops 14192640 | bytes 5474360 | tf_op jit(solution)/shard_map/concatenate | solution.py:35
  70.2 0.0 collective-permute-done.3
  70.3 0.0 copy-done
  70.3 0.0 copy-done.9
  70.3 0.0 copy-done.10
  70.3 7.7 %fusion.3 = bf16[2,64,24,128]{3,1,2,0:T(8,128)(2,1)S(1)} fusion(bf16[6,64,24,128]{3,1,2,0:T(8,128)(2,1)S(1)} %copy-done.2, f32[64,24,128]{2,0,1:T(8,128)S(1)} %convolution_bitcast_fusion, f32[64]{0:T(128)S(1)} %copy-done.9, pred[24]{0:T(512)(128)(4,1)S(1)} %iota_compare_fusion.2, bf16[6,64,28,132]{3,1,2,0:T(8,128)(2,1)S(1)} %constant_dynamic-update-slice_fusion, ...), kind=kOutput, calls=%fused_computation.6 | convolution fusion | flops 86114304 | bytes 23624704 | tf_op jit(solution)/shard_map/oc,zcxy->zoxy/dot_general | solution.py:67
  78.0 1.4 %copy.50 = bf16[2,64,24,128]{3,2,1,0:T(8,128)(2,1)} copy(bf16[2,64,24,128]{3,1,2,0:T(8,128)(2,1)S(1)} %fusion.3) | data formatting | bytes 1572864 | tf_op jit(solution)/shard_map/convert_element_type | solution.py:81
  (6 shorter events, 0.1 us)
Async XLA Ops:
  0.0 70.3 %copy-start = (bf16[64,64]{1,0:T(8,128)(2,1)S(1)}, bf16[64,64]{1,0:T(8,128)(2,1)}, u32[]{:S(2)}) copy-start(bf16[64,64]{1,0:T(8,128)(2,1)} %param.12) | copy-start | bytes 24580
  6.3 8.9 %copy-start.6 = (f32[3,2,128]{2,1,0:T(2,128)S(1)}, f32[3,2,128]{2,1,0:T(2,128)}, u32[]{:S(2)}) copy-start(f32[3,2,128]{2,1,0:T(2,128)} %param.15) | copy-start | bytes 9220
  6.3 22.7 %copy-start.5 = (f32[27,64]{1,0:T(8,128)S(1)}, f32[27,64]{1,0:T(8,128)}, u32[]{:S(2)}) copy-start(f32[27,64]{1,0:T(8,128)} %param.10) | copy-start | bytes 20740
  6.3 22.7 %copy-start.8 = (s32[32]{0:T(128)S(1)}, s32[32]{0:T(128)}, u32[]{:S(2)}) copy-start(s32[32]{0:T(128)} %param.9) | copy-start | bytes 388
  6.3 25.5 %copy-start.1 = (bf16[6,64,24,128]{3,2,1,0:T(8,128)(2,1)S(1)}, bf16[6,64,24,128]{3,2,1,0:T(8,128)(2,1)}, u32[]{:S(2)}) copy-start(bf16[6,64,24,128]{3,2,1,0:T(8,128)(2,1)} %param.8) | copy-start | bytes 7077892
  6.4 31.1 %collective-permute-start = (bf16[6,64,24,2]{1,2,3,0:T(8,128)(2,1)S(1)}, bf16[6,64,24,2]{1,2,3,0:T(8,128)(2,1)S(1)}, u32[]{:S(2)}, u32[]{:S(2)}) collective-permute-start(bf16[6,64,24,2]{1,2,3,0:T(8,128)(2,1)S(1)} %copy.53), channel_id=1, source_target_pairs={{0,1},{1,2},{2,3},{3,4},{4,5},{5,6},{6,7},{7,8},{8,9},{9,10},{10,1... | collective-permute-start | bytes 110600 | tf_op jit(solution)/shard_map/ppermute | solution.py:18
  12.8 26.8 %collective-permute-start.1 = (bf16[6,64,24,2]{1,2,3,0:T(8,128)(2,1)S(1)}, bf16[6,64,24,2]{1,2,3,0:T(8,128)(2,1)S(1)}, u32[]{:S(2)}, u32[]{:S(2)}) collective-permute-start(bf16[6,64,24,2]{1,2,3,0:T(8,128)(2,1)S(1)} %copy.54), channel_id=1, source_target_pairs={{1,0},{2,1},{3,2},{4,3},{5,4},{6,5},{7,6},{8,7},{9,8},{10,9},{11,1... | collective-permute-start | bytes 110600 | tf_op jit(solution)/shard_map/ppermute | solution.py:20
  16.1 20.4 %all-to-all-start = ((f32[3,2,128]{0,1,2:T(2,128)}), f32[3,2,128]{0,1,2:T(2,128)S(1)}, u32[]{:S(2)}, u32[]{:S(2)}) async-start(f32[3,2,128]{0,1,2:T(2,128)} %copy.44), calls=%async_computation | async-start | bytes 262144 | tf_op jit(solution)/shard_map/all_to_all | solution.py:70
  39.6 2.1 %copy-start.2 = (bf16[6,64,24,128]{3,1,2,0:T(8,128)(2,1)S(1)}, bf16[6,64,24,128]{3,1,2,0:T(8,128)(2,1)}, u32[]{:S(2)}) copy-start(bf16[6,64,24,128]{3,1,2,0:T(8,128)(2,1)} %copy.37) | copy-start | bytes 7077892
  41.7 7.0 %copy-start.7 = (f32[64,3]{0,1:T(4,128)S(1)}, f32[64,3]{0,1:T(4,128)}, u32[]{:S(2)}) copy-start(f32[64,3]{0,1:T(4,128)} %param.14) | copy-start | bytes 2308
  41.7 24.4 %copy-start.4 = (bf16[6,64,24,2]{3,1,2,0:T(8,128)(2,1)S(1)}, bf16[6,64,24,2]{3,1,2,0:T(8,128)(2,1)}, u32[]{:S(2)}) copy-start(bf16[6,64,24,2]{3,1,2,0:T(8,128)(2,1)} %copy.42) | copy-start | bytes 110596
  46.5 19.5 %copy-start.3 = (bf16[6,64,24,2]{3,1,2,0:T(8,128)(2,1)S(1)}, bf16[6,64,24,2]{3,1,2,0:T(8,128)(2,1)}, u32[]{:S(2)}) copy-start(bf16[6,64,24,2]{3,1,2,0:T(8,128)(2,1)} %copy.40) | copy-start | bytes 110596
  46.6 19.5 %collective-permute-start.2 = (bf16[6,64,2,132]{3,1,2,0:T(8,128)(2,1)S(1)}, bf16[6,64,2,132]{3,1,2,0:T(8,128)(2,1)S(1)}, u32[]{:S(2)}, u32[]{:S(2)}) collective-permute-start(bf16[6,64,2,132]{3,1,2,0:T(8,128)(2,1)S(1)} %get-tuple-element.6), channel_id=1, source_target_pairs={{0,16},{16,32},{32,48},{48,64},{64,80},{80,96},{96,112},{112,128},... | collective-permute-start | bytes 608264 | tf_op jit(solution)/shard_map/ppermute | solution.py:29
  49.5 20.7 %copy-start.9 = (f32[64]{0:T(128)S(1)}, f32[64]{0:T(128)}, u32[]{:S(2)}) copy-start(f32[64]{0:T(128)} %param.13) | copy-start | bytes 772
  49.5 20.7 %copy-start.10 = (f32[64]{0:T(128)S(1)}, f32[64]{0:T(128)}, u32[]{:S(2)}) copy-start(f32[64]{0:T(128)} %param.11) | copy-start | bytes 772
  49.5 20.7 %collective-permute-start.3 = (bf16[6,64,2,132]{3,1,2,0:T(8,128)(2,1)S(1)}, bf16[6,64,2,132]{3,1,2,0:T(8,128)(2,1)S(1)}, u32[]{:S(2)}, u32[]{:S(2)}) collective-permute-start(bf16[6,64,2,132]{3,1,2,0:T(8,128)(2,1)S(1)} %get-tuple-element.5), channel_id=1, source_target_pairs={{0,496},{16,0},{32,16},{48,32},{64,48},{80,64},{96,80},{112,96},{1... | collective-permute-start | bytes 608264 | tf_op jit(solution)/shard_map/ppermute | solution.py:29
where the time goes:
time: 79.8 us; the launch traced here: 79.4 us
  starting transfers between devices  30.8 us (39%)
  local copies, waits for them, and re-layouts  20 us (25%)
  other arithmetic  10.3 us (13%)
  matrix products  8.73 us (11%)
  waiting for transfers between devices  6.7 us (8%)
  between operations  2.77 us (3%)
    all_to_all x1, starting transfers between devices, shards(): lax.all_to_all(coarse, 'gy', split_axis=2, concat_axis=1, tiled=True)  13 us
    ppermute x2, starting transfers between devices, passed_along(): lax.ppermute(shard, axis, [(i, (i + by) % length) for i in range(length)])  11.9 us
    dot_general x1, matrix products, shards(): jnp.einsum('oc,zcxy->zoxy', pw_weight, depth, preferred_element_type=jnp....  7.71 us
    unnamed x26, local copies, waits for them, and re-layouts  7.25 us
    ppermute x2, waiting for transfers between devices, passed_along(): lax.ppermute(shard, axis, [(i, (i + by) % length) for i in range(length)])  6.7 us
    slice x1, local copies, waits for them, and re-layouts, with_halo(): lax.slice_in_dim(cells, cells.shape[dim] - width, cells.shape[dim], axis=...  4.86 us
    concatenate x1, other arithmetic, with_halo(): jnp.concatenate([lax.ppermute(tail, axis, [(i, (i + 1) % count) for i in...  4.81 us
    concatenate x1, other arithmetic, attach_rows(): jnp.concatenate([from_lower, block, jnp.zeros(rim_shape, block.dtype)], a...  4.1 us
  transfers between devices with their start and end apart: 5, of which 1 were waited for; matrix products, arithmetic and copies ran while one was open for 21% of the time, Pallas kernels for 0%

commit v1 on v0

v1 whole, which is shorter than its diff:
```python
import functools

import jax
import jax.numpy as jnp
from jax import lax
from jax.experimental import pallas as pl
from jax.experimental.pallas import tpu as pltpu
from jax.sharding import PartitionSpec as P

MESH = pl.DeviceIdType.MESH
XW = 16
ZIN = 6
ZOUT = 2
C = 64
CF = 16
SUB = 8
F32 = jnp.float32
BF16 = jnp.bfloat16
HIGH = lax.Precision.HIGHEST
NN = (((1,), (0,)), ((), ()))
NT = (((1,), (1,)), ((), ()))
TN = (((0,), (0,)), ((), ()))


def iota(shape, dim):
    return lax.broadcasted_iota(jnp.int32, shape, dim)


def dot(a, b, dims=NN, precision=None):
    return lax.dot_general(a, b, dims, precision=precision, preferred_element_type=F32)


def tap(dz, dx, dy):
    return 9 * (dz + 1) + 3 * (dx + 1) + (dy + 1)


def depth_kernel(
    nx, ny,
    widths, dw_s, bias_s, dw_v, coarse, feat,
    depth_ref, up_ref,
    field, local, rim, wide, place, stage, rim_edge, edge,
    row_send, row_recv, corn_send, corn_recv, col_send, col_recv, own, coarse_all,
    field_sem, row_ssem, row_rsem, corn_ssem, corn_rsem, col_ssem, col_rsem, co_ssem, co_rsem,
):
    lanes = feat.shape[3]
    blocks = feat.shape[2] // SUB
    block = C * SUB
    gx, gy = lax.axis_index("gx"), lax.axis_index("gy")
    above = lax.rem(gx + 1, nx)
    below = lax.rem(gx + nx - 1, nx)
    sides = (below, above)

    def along(k):
        return lax.rem(gy + k, ny)

    lefts = (along(ny - 1), along(1))

    barrier = pltpu.get_barrier_semaphore()
    for k in range(1, ny):
        pl.semaphore_signal(barrier, inc=1, device_id=(gx, along(k)), device_id_type=MESH)
    for x in sides:
        for y in (gy,) + lefts:
            pl.semaphore_signal(barrier, inc=1, device_id=(x, y), device_id_type=MESH)

    loads = []
    for p in range(ZIN):
        for b in range(blocks):
            loads.append(
                pltpu.make_async_copy(
                    feat.at[p, :, pl.ds(SUB * b, SUB), :], field.at[p, b], field_sem.at[p, b]
                )
            )
            loads[-1].start()

    width = widths[gx]
    start = jnp.int32(0)
    for d in range(nx):
        start = start + jnp.where(d < gx, widths[d], 0)

    rows = coarse.shape[1]
    own[...] = jnp.zeros_like(own)
    for k in range(3):
        own[pl.ds(k * rows, rows), :] = coarse[k]

    eye = (iota((C, C), 0) == iota((C, C), 1)).astype(F32)
    by_channel = dot(eye, dw_v[...], NT, HIGH)
    for side, dx in ((0, 1), (1, -1)):
        for dz in (-1, 0, 1):
            for dy in (-1, 0, 1):
                t = tap(dz, dx, dy)
                wide[side, 3 * (dz + 1) + dy + 1] = jnp.broadcast_to(
                    by_channel[:, t : t + 1], (C, lanes)
                )
    spread = (iota((C, block), 0) == iota((C, block), 1) // SUB).astype(F32)
    by_lane = dot(dw_v[...], spread, NN, HIGH)

    half = C // 2
    pick_row = iota((2 * half, half * SUB), 0)
    pick_col = iota((2 * half, half * SUB), 1)
    same = (pick_row % half) == (pick_col // SUB)

    def picks(first, b):
        hit = same & ((pick_col % SUB) + SUB * b == first + pick_row // half)
        return jnp.where(hit, 1.0, 0.0).astype(BF16)

    pick_top = picks(0, 0)
    pick_bottom = [picks(width - 2, b) for b in range(blocks)]

    for at in range(ZIN * blocks):
        loads[at].wait()

    for p in range(ZIN):
        for h in range(2):
            part = [
                field[p, b, pl.ds(h * half, half)].reshape(half * SUB, lanes) for b in range(blocks)
            ]
            top = dot(pick_top, part[0])
            bottom = dot(pick_bottom[0], part[0])
            for b in range(1, blocks):
                bottom = bottom + dot(pick_bottom[b], part[b])
            for r in range(2):
                rim[0, p, r, pl.ds(h * half, half), :] = top[r * half : (r + 1) * half]
                rim[1, p, r, pl.ds(h * half, half), :] = bottom[r * half : (r + 1) * half]

    lane = iota((C, lanes), 1)
    for side in range(2):
        for z in range(ZOUT):
            for r in range(2):
                sums = [None, None, None]
                for dz in (-1, 0, 1):
                    cells = rim[side, z + 2 + 2 * dz, r]
                    for dy in (-1, 0, 1):
                        term = wide[side, 3 * (dz + 1) + dy + 1] * cells
                        sums[dy + 1] = term if sums[dy + 1] is None else sums[dy + 1] + term
                at = pl.ds(z * 2 * C + r * C, C)
                total = sums[1]
                total = total + jnp.where(lane < lanes - 2, pltpu.roll(sums[2], lanes - 2, 1), 0.0)
                total = total + jnp.where(lane >= 2, pltpu.roll(sums[0], 2, 1), 0.0)
                row_send[side, at, :] = total.astype(BF16)
                rim_edge[side, 0, at, :] = sums[2].astype(BF16)
                rim_edge[side, 1, at, :] = sums[0].astype(BF16)

    pl.semaphore_wait(barrier, ny - 1 + 6)

    copies = []
    for k in range(1, ny):
        copies.append(
            pltpu.make_async_remote_copy(
                src_ref=own, dst_ref=coarse_all.at[gy], send_sem=co_ssem.at[k - 1],
                recv_sem=co_rsem.at[k - 1], device_id=(gx, along(k)), device_id_type=MESH,
            )
        )
        copies[-1].start()
    coarse_all[gy] = own[...]
    for side in range(2):
        copies.append(
            pltpu.make_async_remote_copy(
                src_ref=row_send.at[side], dst_ref=row_recv.at[1 - side],
                send_sem=row_ssem.at[side], recv_sem=row_rsem.at[1 - side],
                device_id=(sides[side], gy), device_id_type=MESH,
            )
        )
        copies[-1].start()

    ends_row, ends_lane = iota((16, lanes), 0), iota((16, lanes), 1)
    ends = [
        jnp.where((ends_row < 2) & (ends_lane == ends_row + first), 1.0, 0.0).astype(BF16)
        for first in (0, lanes - 2)
    ]
    for side in range(2):
        for e in range(2):
            corn_send[side, e] = dot(ends[e], rim_edge[side, e], NT)[:SUB]
    for side in range(2):
        for e in range(2):
            copies.append(
                pltpu.make_async_remote_copy(
                    src_ref=corn_send.at[side, e], dst_ref=corn_recv.at[1 - side, 1 - e],
                    send_sem=corn_ssem.at[side, e], recv_sem=corn_rsem.at[1 - side, 1 - e],
                    device_id=(sides[side], lefts[e]), device_id_type=MESH,
                )
            )
            copies[-1].start()

    both = jnp.where(
        ((ends_row < 2) & (ends_lane == ends_row))
        | ((ends_row >= 2) & (ends_row < 4) & (ends_lane == ends_row + lanes - 4)),
        1.0, 0.0,
    ).astype(BF16)
    in_block = iota((SUB, block), 1) % SUB
    for p in range(ZIN):
        for b in range(blocks):
            found = dot(both, field[p, b].reshape(block, lanes), NT)[:SUB]
            edge[p, b] = jnp.where(in_block + SUB * b < width, found, 0.0)
    first_two = iota((SUB, block), 0) < 2
    weight = {}
    for dz in (-1, 0, 1):
        for dx in (-1, 0, 1):
            high, low = tap(dz, dx, 1), tap(dz, dx, -1)
            weight[dz, dx] = jnp.where(
                first_two,
                jnp.broadcast_to(by_lane[high : high + 1], (SUB, block)),
                jnp.broadcast_to(by_lane[low : low + 1], (SUB, block)),
            )
    for z in range(ZOUT):
        sums = {}
        for dx in (-1, 0, 1):
            for b in range(blocks):
                total = weight[-1, dx] * edge[z, b]
                total = total + weight[0, dx] * edge[z + 2, b]
                sums[dx, b] = total + weight[1, dx] * edge[z + 4, b]
        for b in range(blocks):
            total = sums[0, b]
            total = total + jnp.where(in_block < 6, pltpu.roll(sums[1, b], block - 2, 1), 0.0)
            total = total + jnp.where(in_block >= 2, pltpu.roll(sums[-1, b], 2, 1), 0.0)
            if b + 1 < blocks:
                total = total + jnp.where(in_block >= 6, pltpu.roll(sums[1, b + 1], 6, 1), 0.0)
            if b > 0:
                total = total + jnp.where(
                    in_block < 2, pltpu.roll(sums[-1, b - 1], block - 6, 1), 0.0
                )
            at = pl.ds((z * blocks + b) * block, block)
            col_send[0, :, at] = total[0:2]
            col_send[1, :, at] = total[2:4]
    for e in range(2):
        copies.append(
            pltpu.make_async_remote_copy(
                src_ref=col_send.at[e], dst_ref=col_recv.at[1 - e],
                send_sem=col_ssem.at[e], recv_sem=col_rsem.at[1 - e],
                device_id=(gx, lefts[e]), device_id_type=MESH,
            )
        )
        copies[-1].start()

    stage[...] = jnp.zeros_like(stage)
    slot = iota((2, SUB, lanes), 1)
    line = iota((blocks * SUB, lanes), 1)

    def pair(i, carry):
        c0 = 2 * i
        for p in range(ZIN):
            for b in range(blocks):
                cells = field[p, b, pl.ds(c0, 2)].astype(F32)
                if b > 0:
                    cells = jnp.where(slot + SUB * b < width, cells, 0.0)
                for h in range(2):
                    stage[h, p, pl.ds(SUB * (b + 1), SUB), :] = cells[h]
        for h in range(2):
            for z in range(ZOUT):
                sums = [None, None, None]
                for dz in (-1, 0, 1):
                    for dx in (-1, 0, 1):
                        cells = stage[h, z + 2 + 2 * dz, pl.ds(SUB + 2 * dx, SUB * blocks), :]
                        for dy in (-1, 0, 1):
                            term = dw_s[tap(dz, dx, dy), c0 + h] * cells
                            sums[dy + 1] = term if sums[dy + 1] is None else sums[dy + 1] + term
                total = sums[1] + bias_s[c0 + h]
                total = total + jnp.where(line < lanes - 2, pltpu.roll(sums[2], lanes - 2, 1), 0.0)
                total = total + jnp.where(line >= 2, pltpu.roll(sums[0], 2, 1), 0.0)
                for b in range(blocks):
                    local[z, b, c0 + h] = total[SUB * b : SUB * (b + 1)]
        return carry

    lax.fori_loop(0, C // 2, pair, 0)

    put_row, put_col = iota((block, 4 * C), 0), iota((block, 4 * C), 1)
    alike = (put_row // SUB) == (put_col % C)
    target = jnp.where(put_col < 2 * C, put_col // C, width - 2 + (put_col // C) - 2)
    for b in range(blocks):
        hit = alike & ((put_row % SUB) + SUB * b == target)
        place[b] = jnp.where(hit, 1.0, 0.0).astype(BF16)

    for copy in copies:
        copy.wait_recv()

    ncols = coarse_all.shape[2]
    held = coarse_all[...].reshape(ny * SUB, ncols)
    column = (
        iota((ncols, lanes), 0) == gy * (lanes // CF) + iota((ncols, lanes), 1) // CF
    ).astype(F32)
    count = blocks * SUB
    up_row, up_col = iota((3 * count, ny * SUB), 0), iota((3 * count, ny * SUB), 1)
    cell = start + up_row % count
    cell = jnp.where(cell >= XW * nx, cell - XW * nx, cell) // CF
    hit = (up_col // SUB == cell // rows) & (up_col % SUB == (up_row // count) * rows + cell % rows)
    along_y = dot(held, column, NN, HIGH)
    up_ref[...] = dot(jnp.where(hit, 1.0, 0.0), along_y, NN, HIGH)

    back = [
        jnp.where((iota((SUB, lanes), 0) < 2) & (iota((SUB, lanes), 1) == iota((SUB, lanes), 0) + first), 1.0, 0.0)
        for first in (0, lanes - 2)
    ]
    arrived = []
    for side in range(2):
        total = row_recv[side].astype(F32)
        for e in range(2):
            total = total + dot(corn_recv[side, e].astype(BF16), back[e].astype(BF16), TN)
        arrived.append(total.astype(BF16))
    back_row, back_lane = iota((4, lanes), 0), iota((4, lanes), 1)
    back_cols = jnp.where(
        back_lane == jnp.where(back_row < 2, back_row, back_row + lanes - 4), 1.0, 0.0
    ).astype(BF16)
    for z in range(ZOUT):
        near = jnp.concatenate([arrived[s][2 * C * z : 2 * C * (z + 1)] for s in range(2)], axis=0)
        for b in range(blocks):
            at = pl.ds((z * blocks + b) * block, block)
            cols = jnp.concatenate([col_recv[0, :, at], col_recv[1, :, at]], axis=0)
            total = local[z, b].reshape(block, lanes) + dot(place[b], near)
            total = total + dot(cols.astype(BF16), back_cols, TN)
            depth_ref[z, pl.ds(b * block, block), :] = total.astype(BF16)

    for copy in copies:
        copy.wait_send()


def mix_kernel(
    widths, pwb_s, lift_s, pw_v, up, depth, feat, out, field, mixed, result, in_sem, out_sem
):
    lanes = feat.shape[3]
    blocks = feat.shape[2] // SUB
    block = C * SUB
    loads = []
    for z in range(ZOUT):
        for b in range(blocks):
            loads.append(
                pltpu.make_async_copy(
                    feat.at[ZOUT + z, :, pl.ds(SUB * b, SUB), :], field.at[z, b], in_sem.at[z, b]
                )
            )
            loads[-1].start()
    width = widths[lax.axis_index("gx")]
    tall = (iota((block, C), 0) // SUB == iota((block, C), 1)).astype(BF16)
    flat = (iota((C, block), 1) // SUB == iota((C, block), 0)).astype(BF16)
    full = dot(dot(tall, pw_v[...]).astype(BF16), flat)
    keep = iota((block, block), 0) % SUB == iota((block, block), 1) % SUB
    full = jnp.where(keep, full, 0.0).astype(BF16)
    for b in range(blocks):
        at = pl.ds(b * block, block)
        cells = jnp.concatenate([depth[z, at, :] for z in range(ZOUT)], axis=1)
        mixed[b] = dot(full, cells).reshape(C, SUB, ZOUT * lanes)
    for load in loads:
        load.wait()
    ups = [
        [up[pl.ds(k * blocks * SUB + b * SUB, SUB), :] for b in range(blocks)] for k in range(3)
    ]
    slot = iota((SUB, lanes), 0)

    def pair(i, carry):
        for b in range(blocks):
            lifted = []
            for h in range(2):
                c = 2 * i + h
                total = lift_s[0, c] * ups[0][b] + lift_s[1, c] * ups[1][b] + lift_s[2, c] * ups[2][b]
                lifted.append(total)
            for z in range(ZOUT):
                values = []
                cells = field[z, b, pl.ds(2 * i, 2)].astype(F32)
                for h in range(2):
                    c = 2 * i + h
                    v = mixed[b, c, :, z * lanes : (z + 1) * lanes] + pwb_s[c]
                    v = cells[h] + jnp.where(v > 0, v, 0.2 * v) + lifted[h]
                    values.append(jnp.where(slot + SUB * b < width, v, 0.0))
                result[z, b, pl.ds(2 * i, 2)] = jnp.stack(values).astype(BF16)
        return carry

    parts = 4
    size = C // parts
    stores = []
    for part in range(parts):
        lax.fori_loop(part * size // 2, (part + 1) * size // 2, pair, 0)
        for z in range(ZOUT):
            for b in range(blocks):
                stores.append(
                    pltpu.make_async_copy(
                        result.at[z, b, pl.ds(part * size, size)],
                        out.at[z, pl.ds(part * size, size), pl.ds(SUB * b, SUB), :],
                        out_sem.at[part, z, b],
                    )
                )
                stores[-1].start()
    for store in stores:
        store.wait()


def shards(feature, widths, dw_weight, dw_bias, pw_weight, pw_bias, lift_weight, coarse):
    nx, ny = lax.axis_size("gx"), lax.axis_size("gy")
    slots, lanes = feature.shape[2], feature.shape[3]
    blocks = slots // SUB
    block = C * SUB
    ncols = coarse.shape[2]
    smem = pl.BlockSpec(memory_space=pltpu.SMEM)
    vmem = pl.BlockSpec(memory_space=pltpu.VMEM)
    anyw = pl.BlockSpec(memory_space=pl.ANY)
    dma = pltpu.SemaphoreType.DMA
    depth, up = pl.pallas_call(
        functools.partial(depth_kernel, nx, ny),
        out_shape=(
            jax.ShapeDtypeStruct((ZOUT, blocks * block, lanes), BF16),
            jax.ShapeDtypeStruct((3 * slots, lanes), F32),
        ),
        in_specs=[smem, smem, smem, vmem, vmem, anyw],
        out_specs=(vmem, vmem),
        scratch_shapes=[
            pltpu.VMEM((ZIN, blocks, C, SUB, lanes), BF16),
            pltpu.VMEM((ZOUT, blocks, C, SUB, lanes), F32),
            pltpu.VMEM((2, ZIN, 2, C, lanes), F32),
            pltpu.VMEM((2, 9, C, lanes), F32),
            pltpu.VMEM((blocks, block, 4 * C), BF16),
            pltpu.VMEM((2, ZIN, (blocks + 2) * SUB, lanes), F32),
            pltpu.VMEM((2, 2, ZOUT * 2 * C, lanes), BF16),
            pltpu.VMEM((ZIN, blocks, SUB, block), F32),
            pltpu.VMEM((2, ZOUT * 2 * C, lanes), BF16),
            pltpu.VMEM((2, ZOUT * 2 * C, lanes), BF16),
            pltpu.VMEM((2, 2, SUB, ZOUT * 2 * C), F32),
            pltpu.VMEM((2, 2, SUB, ZOUT * 2 * C), F32),
            pltpu.VMEM((2, 2, ZOUT * blocks * block), F32),
            pltpu.VMEM((2, 2, ZOUT * blocks * block), F32),
            pltpu.VMEM((SUB, ncols), F32),
            pltpu.VMEM((ny, SUB, ncols), F32),
            dma((ZIN, blocks)),
            dma((2,)), dma((2,)), dma((2, 2)), dma((2, 2)), dma((2,)), dma((2,)),
            dma((ny - 1,)), dma((ny - 1,)),
        ],
        compiler_params=pltpu.CompilerParams(collective_id=0, has_side_effects=True),
        name="depth",
    )(widths, dw_weight, dw_bias, dw_weight, coarse, feature)
    return pl.pallas_call(
        mix_kernel,
        out_shape=jax.ShapeDtypeStruct((ZOUT, C, slots, lanes), BF16),
        in_specs=[smem, smem, smem, vmem, vmem, vmem, anyw],
        out_specs=anyw,
        scratch_shapes=[
            pltpu.VMEM((ZOUT, blocks, C, SUB, lanes), BF16),
            pltpu.VMEM((blocks, C, SUB, ZOUT * lanes), F32),
            pltpu.VMEM((ZOUT, blocks, C, SUB, lanes), BF16),
            dma((ZOUT, blocks)),
            dma((4, ZOUT, blocks)),
        ],
        name="mix",
    )(widths, pw_bias, lift_weight.T, pw_weight, up, depth, feature)


def solution(mesh):
    placed = (P(None, None, "gx", "gy"), P(), P(), P(), P(), P(), P(), P(None, "gy", None))
    return jax.shard_map(
        shards, mesh=mesh, in_specs=placed, out_specs=P(None, None, "gx", "gy"), check_vma=False
    )
```

time: 79.8 us -> 31.3 us (0.39)
  the two profiles are of different devices: /device:TPU:14 before, /device:TPU:1 now
where the time goes in v1:
time: 31.3 us; the launch traced here: 31 us
  Pallas kernels  31 us (99%)
    pallas_call x1, Pallas kernels, shards(): pl.pallas_call(functools.partial(depth_kernel, nx, ny), out_shape=(jax.Sh...  26.7 us
    pallas_call x1, Pallas kernels, shards(): pl.pallas_call(mix_kernel, out_shape=jax.ShapeDtypeStruct((ZOUT, C, slots...  4.36 us

profile of v1, /device:TPU:1, one launch (start us, length us, event | category | flops | bytes accessed | tf_op | source)
XLA Modules:
  0.0 31.0 jit_solution(12288600328159133800)
XLA Ops:
  0.0 26.7 %depth.1 = (bf16[2,1536,128]{2,1,0:T(8,128)(2,1)}, f32[72,128]{1,0:T(8,128)}) custom-call(s32[32]{0:T(128)} %widths.3, f32[27,64]{1,0:T(8,128)} %dw_v.1, f32[64]{0:T(128)} %bias_s.1, f32[27,64]{1,0:T(8,128)} %dw_v.1, f32[3,2,128]{2,1,0:T(2,128)} %coarse.1, bf16[6,64,24,128]{3,2,1,0:T(8,128)(2,1)} %feat.3), custom_call_target="tpu_custom_call" | custom-call | tf_op jit(solution)/shard_map/depth/pallas_call | solution.py:394
  26.7 4.4 %mix.1 = bf16[2,64,24,128]{3,2,1,0:T(8,128)(2,1)} custom-call(s32[32]{0:T(128)} %widths.3, f32[64]{0:T(128)} %pwb_s.1, f32[3,64]{1,0:T(4,128)} %bitcast.1, bf16[64,64]{1,0:T(8,128)(2,1)} %pw_v.1, f32[72,128]{1,0:T(8,128)} %get-tuple-element.7.up, bf16[2,1536,128]{2,1,0:T(8,128)(2,1)} %get-tuple-element.8.depth, bf16[6,64,24,128]{3,2,1,0:T(8,128)(2,1)} %feat.3), custom_call_target="tpu_custom_call" | custom-call | tf_op jit(solution)/shard_map/mix/pallas_call | solution.py:426

commit v2 on v1

v2 whole, which is shorter than its diff:
```python
import functools

import jax
import jax.numpy as jnp
from jax import lax
from jax.experimental import pallas as pl
from jax.experimental.pallas import tpu as pltpu
from jax.sharding import PartitionSpec as P

MESH = pl.DeviceIdType.MESH
XW = 16
ZIN = 6
ZOUT = 2
C = 64
CF = 16
VMEM_LIMIT = 50000 * 1024
SUB = 8
F32 = jnp.float32
BF16 = jnp.bfloat16
HIGH = lax.Precision.HIGHEST
NN = (((1,), (0,)), ((), ()))
NT = (((1,), (1,)), ((), ()))
TN = (((0,), (0,)), ((), ()))


def iota(shape, dim):
    return lax.broadcasted_iota(jnp.int32, shape, dim)


def dot(a, b, dims=NN, precision=None):
    return lax.dot_general(a, b, dims, precision=precision, preferred_element_type=F32)


def tap(dz, dx, dy):
    return 9 * (dz + 1) + 3 * (dx + 1) + (dy + 1)


def block_kernel(
    nx, ny,
    widths_h, dw_h, dwb_h, pw_h, pwb_h, lift_h, coarse_h, feat,
    out,
    widths, dw_s, bias_s, pwb_s, lift_s, dw_v, pw_v, coarse,
    field, local, mixed, base, result, rim, wide, near_w, stage, rim_edge, edge,
    row_send, row_recv, corn_send, corn_recv, col_send, col_recv, own, coarse_all,
    arg_sem, field_sem, row_ssem, row_rsem, corn_ssem, corn_rsem, col_ssem, col_rsem,
    co_ssem, co_rsem, out_sem,
):
    lanes = feat.shape[3]
    blocks = feat.shape[2] // SUB
    block = C * SUB
    gx, gy = lax.axis_index("gx"), lax.axis_index("gy")
    sides = (lax.rem(gx + nx - 1, nx), lax.rem(gx + 1, nx))

    def along(k):
        return lax.rem(gy + k, ny)

    lefts = (along(ny - 1), along(1))

    given = (
        (widths_h, widths), (dw_h, dw_v), (dw_h, dw_s), (coarse_h, coarse), (dwb_h, bias_s),
        (pwb_h, pwb_s), (lift_h, lift_s), (pw_h, pw_v),
    )
    fetch = [pltpu.make_async_copy(a, b, arg_sem.at[i]) for i, (a, b) in enumerate(given)]
    for copy in fetch[:4]:
        copy.start()
    loads = []
    for p in range(ZIN):
        for b in range(blocks):
            loads.append(
                pltpu.make_async_copy(
                    feat.at[p, :, pl.ds(SUB * b, SUB), :], field.at[p, b], field_sem.at[p, b]
                )
            )
            loads[-1].start()

    barrier = pltpu.get_barrier_semaphore()
    for x in sides:
        for y in (gy,) + lefts:
            pl.semaphore_signal(barrier, inc=1, device_id=(x, y), device_id_type=MESH)
    for k in range(1, ny):
        pl.semaphore_signal(barrier, inc=1, device_id=(gx, along(k)), device_id_type=MESH)
    for copy in fetch[4:]:
        copy.start()
    for copy in fetch[:4]:
        copy.wait()
    width = widths[gx]

    def send(src, dst, ssem, rsem, to):
        return pltpu.make_async_remote_copy(
            src_ref=src, dst_ref=dst, send_sem=ssem, recv_sem=rsem, device_id=to,
            device_id_type=MESH,
        )

    rows_out = [
        send(
            row_send.at[s], row_recv.at[1 - s], row_ssem.at[s], row_rsem.at[1 - s], (sides[s], gy)
        )
        for s in range(2)
    ]
    corners_out = [
        send(
            corn_send.at[s, e], corn_recv.at[1 - s, 1 - e], corn_ssem.at[s, e],
            corn_rsem.at[1 - s, 1 - e], (sides[s], lefts[e]),
        )
        for s in range(2) for e in range(2)
    ]
    cols_out = [
        send(col_send.at[e], col_recv.at[1 - e], col_ssem.at[e], col_rsem.at[1 - e], (gx, lefts[e]))
        for e in range(2)
    ]
    coarse_out = [
        send(own, coarse_all.at[gy], co_ssem.at[k - 1], co_rsem.at[k - 1], (gx, along(k)))
        for k in range(1, ny)
    ]
    last = lax.rem(gx, nx // 2 if nx % 2 == 0 else nx) == 0
    soon = jnp.logical_not(last)

    def meet():
        pl.semaphore_wait(barrier, ny - 1 + 6)

    rows = coarse.shape[1]
    own[...] = jnp.zeros_like(own)
    for k in range(3):
        own[pl.ds(k * rows, rows), :] = coarse[k]
    coarse_all[gy] = own[...]

    eye = (iota((C, C), 0) == iota((C, C), 1)).astype(F32)
    by_channel = dot(eye, dw_v[...], NT, HIGH)
    for side, dx in ((1, -1), (0, 1)):
        for dz in (-1, 0, 1):
            for dy in (-1, 0, 1):
                t = tap(dz, dx, dy)
                wide[side, 3 * (dz + 1) + dy + 1] = jnp.broadcast_to(
                    by_channel[:, t : t + 1], (C, lanes)
                )

    half = C // 2
    pick_row = iota((2 * half, half * SUB), 0)
    pick_col = iota((2 * half, half * SUB), 1)
    same = (pick_row % half) == (pick_col // SUB)

    def picks(first, b):
        hit = same & ((pick_col % SUB) + SUB * b == first + pick_row // half)
        return jnp.where(hit, 1.0, 0.0).astype(BF16)

    pick_rim = [picks(0, 0), jnp.concatenate([picks(width - 2, b) for b in range(blocks)], axis=1)]
    lane = iota((C, lanes), 1)
    ends_row, ends_lane = iota((16, lanes), 0), iota((16, lanes), 1)
    ends = [
        jnp.where(
            (ends_row // 2 == 1 - e) & (ends_lane == ends_row % 2 + e * (lanes - 2)), 1.0, 0.0
        ).astype(BF16)
        for e in range(2)
    ]
    for side in (1, 0):
        for p in range(ZIN):
            if side == 1:
                for b in range(blocks):
                    loads[p * blocks + b].wait()
            for h in range(2):
                part = [
                    field[p, b, pl.ds(h * half, half)].reshape(half * SUB, lanes)
                    for b in range(blocks if side == 1 else 1)
                ]
                found = dot(pick_rim[side], jnp.concatenate(part, axis=0) if side == 1 else part[0])
                for r in range(2):
                    rim[side, p, r, pl.ds(h * half, half), :] = found[r * half : (r + 1) * half]
        for z in range(ZOUT):
            for r in range(2):
                sums = [None, None, None]
                for dz in (-1, 0, 1):
                    cells = rim[side, z + 2 + 2 * dz, r]
                    for dy in (-1, 0, 1):
                        term = wide[side, 3 * (dz + 1) + dy + 1] * cells
                        sums[dy + 1] = term if sums[dy + 1] is None else sums[dy + 1] + term
                total = sums[1]
                total = total + jnp.where(lane < lanes - 2, pltpu.roll(sums[2], lanes - 2, 1), 0.0)
                total = total + jnp.where(lane >= 2, pltpu.roll(sums[0], 2, 1), 0.0)
                row_send[side, pl.ds(r * C, C), pl.ds(z * lanes, lanes)] = total.astype(BF16)
                at = pl.ds(z * 2 * C + r * C, C)
                rim_edge[side, 0, at, :] = sums[2].astype(BF16)
                rim_edge[side, 1, at, :] = sums[0].astype(BF16)
        if side == 1:
            @pl.when(soon)
            def _():
                meet()
                rows_out[1].start()
                for copy in coarse_out:
                    copy.start()

        for e in range(2):
            corn_send[side, e] = dot(ends[e], rim_edge[side, e], NT)[:SUB]

    @pl.when(soon)
    def _():
        rows_out[0].start()
        for copy in corners_out:
            copy.start()

    spread = (iota((C, block), 0) == iota((C, block), 1) // SUB).astype(F32)
    by_lane = dot(dw_v[...], spread, NN, HIGH)
    both = jnp.where(
        ((ends_row < 2) & (ends_lane == ends_row))
        | ((ends_row >= 2) & (ends_row < 4) & (ends_lane == ends_row + lanes - 4)),
        1.0, 0.0,
    ).astype(BF16)
    in_block = iota((SUB, block), 1) % SUB
    for p in range(ZIN):
        for b in range(blocks):
            found = dot(both, field[p, b].reshape(block, lanes), NT)[:SUB]
            edge[p, b] = jnp.where(in_block + SUB * b < width, found, 0.0)
    first_two = iota((SUB, block), 0) < 2
    weight = {}
    for dz in (-1, 0, 1):
        for dx in (-1, 0, 1):
            high, low = tap(dz, dx, 1), tap(dz, dx, -1)
            weight[dz, dx] = jnp.where(
                first_two,
                jnp.broadcast_to(by_lane[high : high + 1], (SUB, block)),
                jnp.broadcast_to(by_lane[low : low + 1], (SUB, block)),
            )
    col_send[...] = jnp.zeros_like(col_send)
    for z in range(ZOUT):
        sums = {}
        for dx in (-1, 0, 1):
            for b in range(blocks):
                total = weight[-1, dx] * edge[z, b]
                total = total + weight[0, dx] * edge[z + 2, b]
                sums[dx, b] = total + weight[1, dx] * edge[z + 4, b]
        for b in range(blocks):
            total = sums[0, b]
            total = total + jnp.where(in_block < 6, pltpu.roll(sums[1, b], block - 2, 1), 0.0)
            total = total + jnp.where(in_block >= 2, pltpu.roll(sums[-1, b], 2, 1), 0.0)
            if b + 1 < blocks:
                total = total + jnp.where(in_block >= 6, pltpu.roll(sums[1, b + 1], 6, 1), 0.0)
            if b > 0:
                total = total + jnp.where(
                    in_block < 2, pltpu.roll(sums[-1, b - 1], block - 6, 1), 0.0
                )
            at = pl.ds(2 * (z * blocks + b), 2)
            col_send[0, at, :] = total[0:2]
            col_send[1, at, :] = total[2:4]
    @pl.when(soon)
    def _():
        for copy in cols_out:
            copy.start()

    for copy in fetch[4:]:
        copy.wait()
    stage[...] = jnp.zeros_like(stage)
    slot = iota((2, SUB, lanes), 1)
    line = iota((blocks * SUB, lanes), 1)

    def taps(i, carry):
        c0 = 2 * i
        for p in range(ZIN):
            for b in range(blocks):
                cells = field[p, b, pl.ds(c0, 2)].astype(F32)
                if b > 0:
                    cells = jnp.where(slot + SUB * b < width, cells, 0.0)
                for h in range(2):
                    stage[h, p, pl.ds(SUB * (b + 1), SUB), :] = cells[h]
        for z in range(ZOUT):
            totals = []
            for h in range(2):
                sums = [None, None, None]
                for dz in (-1, 0, 1):
                    for dx in (-1, 0, 1):
                        cells = stage[h, z + 2 + 2 * dz, pl.ds(SUB + 2 * dx, SUB * blocks), :]
                        for dy in (-1, 0, 1):
                            term = dw_s[tap(dz, dx, dy), c0 + h] * cells
                            sums[dy + 1] = term if sums[dy + 1] is None else sums[dy + 1] + term
                total = sums[1] + bias_s[c0 + h]
                total = total + jnp.where(line < lanes - 2, pltpu.roll(sums[2], lanes - 2, 1), 0.0)
                total = total + jnp.where(line >= 2, pltpu.roll(sums[0], 2, 1), 0.0)
                totals.append(total)
            for b in range(blocks):
                pair = jnp.stack([total[SUB * b : SUB * (b + 1)] for total in totals])
                local[b, pl.ds(c0, 2), :, pl.ds(z * lanes, lanes)] = pair.astype(BF16)
        return carry

    lax.fori_loop(0, C // 2, taps, 0)

    tall = (iota((block, C), 0) // SUB == iota((block, C), 1)).astype(BF16)
    wide_mix = dot(tall, pw_v[...]).astype(BF16)
    flat = (iota((C, block), 1) // SUB == iota((C, block), 0)).astype(BF16)
    keep = iota((block, block), 0) % SUB == iota((block, block), 1) % SUB
    full = jnp.where(keep, dot(wide_mix, flat), 0.0).astype(BF16)
    for b in range(blocks):
        mixed[b] = dot(full, local[b].reshape(block, ZOUT * lanes)).reshape(C, SUB, ZOUT * lanes)
    four = (iota((C, 4 * C), 1) % C == iota((C, 4 * C), 0)).astype(BF16)
    arriving = dot(wide_mix, four)
    put_row, put_col = iota((block, 4 * C), 0), iota((block, 4 * C), 1)
    target = jnp.where(put_col < 2 * C, put_col // C, width - 4 + put_col // C)
    for b in range(blocks):
        hit = (put_row % SUB) + SUB * b == target
        near_w[b] = jnp.where(hit, arriving, 0.0).astype(BF16)

    @pl.when(last)
    def _():
        meet()
        for copy in rows_out[::-1] + coarse_out + corners_out + cols_out:
            copy.start()

    for copy in coarse_out:
        copy.wait_recv()
    start = jnp.int32(0)
    for d in range(nx):
        start = start + jnp.where(d < gx, widths[d], 0)
    ncols = coarse_all.shape[2]
    held = coarse_all[...].reshape(ny * SUB, ncols)
    column = (
        iota((ncols, lanes), 0) == gy * (lanes // CF) + iota((ncols, lanes), 1) // CF
    ).astype(F32)
    count = blocks * SUB
    up_row, up_col = iota((3 * count, ny * SUB), 0), iota((3 * count, ny * SUB), 1)
    cell = start + up_row % count
    cell = jnp.where(cell >= XW * nx, cell - XW * nx, cell) // CF
    hit = (up_col // SUB == cell // rows) & (up_col % SUB == (up_row // count) * rows + cell % rows)
    along_y = dot(held, column, NN, HIGH)
    up = dot(jnp.where(hit, 1.0, 0.0), along_y, NN, HIGH)
    ups = [
        [up[k * count + b * SUB : k * count + (b + 1) * SUB] for b in range(blocks)] for k in range(3)
    ]

    def ready(i, carry):
        for b in range(blocks):
            lifted = []
            for h in range(2):
                c = 2 * i + h
                total = lift_s[0, c] * ups[0][b] + lift_s[1, c] * ups[1][b]
                lifted.append(total + lift_s[2, c] * ups[2][b])
            for z in range(ZOUT):
                at = pl.ds(z * lanes, lanes)
                cells = field[ZOUT + z, b, pl.ds(2 * i, 2)].astype(F32)
                for h in range(2):
                    c = 2 * i + h
                    base[b, c, :, at] = cells[h] + lifted[h]
                    mixed[b, c, :, at] = mixed[b, c, :, at] + pwb_s[c]
        return carry

    lax.fori_loop(0, C // 2, ready, 0)

    back_row, back_lane = iota((SUB, lanes), 0), iota((SUB, lanes), 1)
    back = jnp.where(
        (back_row < 4)
        & (back_lane == jnp.where(back_row < 2, back_row, back_row + lanes - 4)),
        1.0, 0.0,
    ).astype(BF16)
    ends_k, ends_l = iota((32, ZOUT * lanes), 0), iota((32, ZOUT * lanes), 1)
    spot = ends_l % lanes - (ends_k // 16) * (lanes - 2)

    for copy in corners_out + cols_out:
        copy.wait_recv()
    cols = jnp.concatenate([col_recv[0], col_recv[1]], axis=0).astype(BF16)
    mixed_cols = dot(full, cols, NT).astype(BF16)
    corners = [
        dot((corn_recv[side, 0] + corn_recv[side, 1]).astype(BF16), back, TN) for side in range(2)
    ]
    for copy in rows_out:
        copy.wait_recv()
    arrived = []
    for side in range(2):
        parts = [
            row_recv[side, :, pl.ds(z * lanes, lanes)].astype(F32)
            + corners[side][2 * C * z : 2 * C * (z + 1)]
            for z in range(ZOUT)
        ]
        arrived.append(jnp.concatenate(parts, axis=1).astype(BF16))
    stores = []
    for b in range(blocks):
        at_lane = (ends_k % 16) // 2 == (ends_l // lanes) * blocks + b
        pick = jnp.where(at_lane & (spot == ends_k % 2), 1.0, 0.0).astype(BF16)
        right = jnp.concatenate(arrived + [pick], axis=0)
        row_id = iota((block, ZOUT * lanes), 0) % SUB + SUB * b
        v = dot(jnp.concatenate([near_w[b], mixed_cols], axis=1), right)
        v = v + mixed[b].reshape(block, ZOUT * lanes)
        v = base[b].reshape(block, ZOUT * lanes) + jnp.where(v > 0, v, 0.2 * v)
        v = jnp.where(row_id < width, v, 0.0).astype(BF16)
        for z in range(ZOUT):
            result[z, b] = v[:, z * lanes : (z + 1) * lanes].reshape(C, SUB, lanes)
            stores.append(
                pltpu.make_async_copy(
                    result.at[z, b], out.at[z, :, pl.ds(SUB * b, SUB), :], out_sem.at[z, b]
                )
            )
            stores[-1].start()

    for copy in rows_out + corners_out + cols_out + coarse_out:
        copy.wait_send()
    for store in stores:
        store.wait()


def shards(feature, widths, dw_weight, dw_bias, pw_weight, pw_bias, lift_weight, coarse):
    nx, ny = lax.axis_size("gx"), lax.axis_size("gy")
    slots, lanes = feature.shape[2], feature.shape[3]
    blocks = slots // SUB
    block = C * SUB
    both = ZOUT * lanes
    ncols = coarse.shape[2]
    lift = lift_weight.T
    dma = pltpu.SemaphoreType.DMA
    vmem, smem = pltpu.VMEM, pltpu.SMEM
    return pl.pallas_call(
        functools.partial(block_kernel, nx, ny),
        out_shape=jax.ShapeDtypeStruct((ZOUT, C, slots, lanes), BF16),
        in_specs=[pl.BlockSpec(memory_space=pltpu.HBM)] * 8,
        out_specs=pl.BlockSpec(memory_space=pl.ANY),
        scratch_shapes=[
            smem(widths.shape, jnp.int32),
            smem(dw_weight.shape, F32),
            smem(dw_bias.shape, F32),
            smem(pw_bias.shape, F32),
            smem(lift.shape, F32),
            vmem(dw_weight.shape, F32),
            vmem(pw_weight.shape, BF16),
            vmem(coarse.shape, F32),
            vmem((ZIN, blocks, C, SUB, lanes), BF16),
            vmem((blocks, C, SUB, both), BF16),
            vmem((blocks, C, SUB, both), F32),
            vmem((blocks, C, SUB, both), F32),
            vmem((ZOUT, blocks, C, SUB, lanes), BF16),
            vmem((2, ZIN, 2, C, lanes), F32),
            vmem((2, 9, C, lanes), F32),
            vmem((blocks, block, 4 * C), BF16),
            vmem((2, ZIN, (blocks + 2) * SUB, lanes), F32),
            vmem((2, 2, ZOUT * 2 * C, lanes), BF16),
            vmem((ZIN, blocks, SUB, block), F32),
            vmem((2, 2 * C, both), BF16),
            vmem((2, 2 * C, both), BF16),
            vmem((2, 2, SUB, ZOUT * 2 * C), F32),
            vmem((2, 2, SUB, ZOUT * 2 * C), F32),
            vmem((2, 16, block), F32),
            vmem((2, 16, block), F32),
            vmem((SUB, ncols), F32),
            vmem((ny, SUB, ncols), F32),
            dma((8,)),
            dma((ZIN, blocks)),
            dma((2,)), dma((2,)), dma((2, 2)), dma((2, 2)), dma((2,)), dma((2,)),
            dma((ny - 1,)), dma((ny - 1,)),
            dma((ZOUT, blocks)),
        ],
        compiler_params=pltpu.CompilerParams(
            collective_id=0, has_side_effects=True, vmem_limit_bytes=VMEM_LIMIT
        ),
        name="block",
    )(
        *[
            pltpu.with_memory_space_constraint(a, pltpu.HBM)
            for a in (widths, dw_weight, dw_bias, pw_weight, pw_bias, lift, coarse, feature)
        ]
    )


def solution(mesh):
    placed = (P(None, None, "gx", "gy"), P(), P(), P(), P(), P(), P(), P(None, "gy", None))
    return jax.shard_map(
        shards, mesh=mesh, in_specs=placed, out_specs=P(None, None, "gx", "gy"), check_vma=False
    )
```

time: 31.3 us -> 26.4 us (0.84)
  the two profiles are of different devices: /device:TPU:1 before, /device:TPU:8 now
where the time goes in v2:
time: 26.4 us; the launch traced here: 26.2 us
  Pallas kernels  25.3 us (96%)
  local copies, waits for them, and re-layouts  0.88 us (3%)
    pallas_call x1, Pallas kernels, shards(): pl.pallas_call(functools.partial(block_kernel, nx, ny), out_shape=jax.Sha...  25.3 us
    unnamed x1, local copies, waits for them, and re-layouts  0.88 us

profile of v2, /device:TPU:8, one launch (start us, length us, event | category | flops | bytes accessed | tf_op | source)
XLA Modules:
  0.0 26.2 jit_solution(3143017347926365494)
XLA Ops:
  0.0 25.3 %block.1 = bf16[2,64,24,128]{3,2,1,0:T(8,128)(2,1)S(1)} custom-call(s32[32]{0:T(128)} %widths_h.1, f32[27,64]{1,0:T(8,128)} %dw_h.1, f32[64]{0:T(128)} %dwb_h.1, bf16[64,64]{1,0:T(8,128)(2,1)} %pw_h.1, f32[64]{0:T(128)} %pwb_h.1, f32[3,64]{1,0:T(4,128)} %bitcast.1, f32[3,2,128]{2,1,0:T(2,128)} %coarse_h.1, bf16[6,64,24,128]{3,2,1,0:T(8,128)(2,1)} %feat.1), custom_call_target="tpu_custom_call" | custom-call | tf_op jit(solution)/shard_map/block/pallas_call | solution.py:405
  25.3 0.9 %copy.10 = bf16[2,64,24,128]{3,2,1,0:T(8,128)(2,1)} copy(bf16[2,64,24,128]{3,2,1,0:T(8,128)(2,1)S(1)} %block.1) | data formatting | bytes 1572864

commit v3 on v2

--- a/solution.py
+++ b/solution.py
@@ -43,7 +43,7 @@
     field, local, mixed, base, result, rim, wide, near_w, stage, rim_edge, edge,
     row_send, row_recv, corn_send, corn_recv, col_send, col_recv, own, coarse_all,
     arg_sem, field_sem, row_ssem, row_rsem, corn_ssem, corn_rsem, col_ssem, col_rsem,
-    co_ssem, co_rsem, out_sem,
+    co_ssem, co_rsem, out_sem, here,
 ):
     lanes = feat.shape[3]
     blocks = feat.shape[2] // SUB
@@ -74,9 +74,16 @@
             loads[-1].start()
 
     barrier = pltpu.get_barrier_semaphore()
-    for x in sides:
+    span = nx // 2 if nx % 2 == 0 else nx
+    first = lax.rem(gx, span) == 0
+    for y in (gy,) + lefts:
+        pl.semaphore_signal(barrier, inc=1, device_id=(sides[0], y), device_id_type=MESH)
+
+    @pl.when(lax.rem(gx, span) != span - 1)
+    def _():
         for y in (gy,) + lefts:
-            pl.semaphore_signal(barrier, inc=1, device_id=(x, y), device_id_type=MESH)
+            pl.semaphore_signal(barrier, inc=1, device_id=(sides[1], y), device_id_type=MESH)
+
     for k in range(1, ny):
         pl.semaphore_signal(barrier, inc=1, device_id=(gx, along(k)), device_id_type=MESH)
     for copy in fetch[4:]:
@@ -112,12 +119,6 @@
         send(own, coarse_all.at[gy], co_ssem.at[k - 1], co_rsem.at[k - 1], (gx, along(k)))
         for k in range(1, ny)
     ]
-    last = lax.rem(gx, nx // 2 if nx % 2 == 0 else nx) == 0
-    soon = jnp.logical_not(last)
-
-    def meet():
-        pl.semaphore_wait(barrier, ny - 1 + 6)
-
     rows = coarse.shape[1]
     own[...] = jnp.zeros_like(own)
     for k in range(3):
@@ -181,21 +182,29 @@
                 rim_edge[side, 0, at, :] = sums[2].astype(BF16)
                 rim_edge[side, 1, at, :] = sums[0].astype(BF16)
         if side == 1:
-            @pl.when(soon)
+            pl.semaphore_wait(barrier, jnp.where(first, ny - 1 + 3, ny - 1 + 6))
+            rows_out[1].start()
+
+            @pl.when(lax.rem(gx, span) == span - 1)
             def _():
-                meet()
-                rows_out[1].start()
-                for copy in coarse_out:
-                    copy.start()
+                for y in (gy,) + lefts:
+                    pl.semaphore_signal(here, inc=1, device_id=(sides[1], y), device_id_type=MESH)
+
 
         for e in range(2):
             corn_send[side, e] = dot(ends[e], rim_edge[side, e], NT)[:SUB]
 
-    @pl.when(soon)
+    for copy in corners_out[2:]:
+        copy.start()
+
+    @pl.when(jnp.logical_not(first))
     def _():
         rows_out[0].start()
-        for copy in corners_out:
+        for copy in corners_out[:2]:
             copy.start()
+
+    for copy in coarse_out:
+        copy.start()
 
     spread = (iota((C, block), 0) == iota((C, block), 1) // SUB).astype(F32)
     by_lane = dot(dw_v[...], spread, NN, HIGH)
@@ -240,10 +249,8 @@
             at = pl.ds(2 * (z * blocks + b), 2)
             col_send[0, at, :] = total[0:2]
             col_send[1, at, :] = total[2:4]
-    @pl.when(soon)
-    def _():
-        for copy in cols_out:
-            copy.start()
+    for copy in cols_out:
+        copy.start()
 
     for copy in fetch[4:]:
         copy.wait()
@@ -296,12 +303,6 @@
         hit = (put_row % SUB) + SUB * b == target
         near_w[b] = jnp.where(hit, arriving, 0.0).astype(BF16)
 
-    @pl.when(last)
-    def _():
-        meet()
-        for copy in rows_out[::-1] + coarse_out + corners_out + cols_out:
-            copy.start()
-
     for copy in coarse_out:
         copy.wait_recv()
     start = jnp.int32(0)
@@ -349,6 +350,13 @@
     ).astype(BF16)
     ends_k, ends_l = iota((32, ZOUT * lanes), 0), iota((32, ZOUT * lanes), 1)
     spot = ends_l % lanes - (ends_k // 16) * (lanes - 2)
+
+    @pl.when(first)
+    def _():
+        pl.semaphore_wait(here, 3)
+        rows_out[0].start()
+        for copy in corners_out[:2]:
+            copy.start()
 
     for copy in corners_out + cols_out:
         copy.wait_recv()
@@ -440,6 +448,7 @@
             dma((2,)), dma((2,)), dma((2, 2)), dma((2, 2)), dma((2,)), dma((2,)),
             dma((ny - 1,)), dma((ny - 1,)),
             dma((ZOUT, blocks)),
+            pltpu.SemaphoreType.REGULAR,
         ],
         compiler_params=pltpu.CompilerParams(
             collective_id=0, has_side_effects=True, vmem_limit_bytes=VMEM_LIMIT

time: 26.4 us -> 25 us (0.947)
  Pallas kernels: 25.3 us -> 24 us
    pallas_call x1, Pallas kernels: 25.3 us -> 24 us  [shards(): pl.pallas_call(functools.partial(block_kernel, nx, ny), out_shape=jax.Sha...]
where the time goes in v3:
time: 25 us; the launch traced here: 24.9 us
  Pallas kernels  24 us (96%)
  local copies, waits for them, and re-layouts  0.88 us (4%)
    pallas_call x1, Pallas kernels, shards(): pl.pallas_call(functools.partial(block_kernel, nx, ny), out_shape=jax.Sha...  24 us
    unnamed x1, local copies, waits for them, and re-layouts  0.88 us

profile of v3, /device:TPU:8, one launch (start us, length us, event | category | flops | bytes accessed | tf_op | source)
XLA Modules:
  0.0 24.9 jit_solution(7492521409781327819)
XLA Ops:
  0.0 24.0 %block.1 = bf16[2,64,24,128]{3,2,1,0:T(8,128)(2,1)S(1)} custom-call(s32[32]{0:T(128)} %widths_h.1, f32[27,64]{1,0:T(8,128)} %dw_h.1, f32[64]{0:T(128)} %dwb_h.1, bf16[64,64]{1,0:T(8,128)(2,1)} %pw_h.1, f32[64]{0:T(128)} %pwb_h.1, f32[3,64]{1,0:T(4,128)} %bitcast.1, f32[3,2,128]{2,1,0:T(2,128)} %coarse_h.1, bf16[6,64,24,128]{3,2,1,0:T(8,128)(2,1)} %feat.1), custom_call_target="tpu_custom_call" | custom-call | tf_op jit(solution)/shard_map/block/pallas_call | solution.py:413
  24.0 0.9 %copy.10 = bf16[2,64,24,128]{3,2,1,0:T(8,128)(2,1)} copy(bf16[2,64,24,128]{3,2,1,0:T(8,128)(2,1)S(1)} %block.1) | data formatting | bytes 1572864

commit v4 on v3

--- a/solution.py
+++ b/solution.py
@@ -63,15 +63,14 @@
     fetch = [pltpu.make_async_copy(a, b, arg_sem.at[i]) for i, (a, b) in enumerate(given)]
     for copy in fetch[:4]:
         copy.start()
-    loads = []
-    for p in range(ZIN):
+    planes = [[z + 2 * k for k in range(3)] for z in range(ZOUT)]
+    loads = {}
+    for p in planes[0] + planes[1]:
         for b in range(blocks):
-            loads.append(
-                pltpu.make_async_copy(
-                    feat.at[p, :, pl.ds(SUB * b, SUB), :], field.at[p, b], field_sem.at[p, b]
-                )
+            loads[p, b] = pltpu.make_async_copy(
+                feat.at[p, :, pl.ds(SUB * b, SUB), :], field.at[p, b], field_sem.at[p, b]
             )
-            loads[-1].start()
+            loads[p, b].start()
 
     barrier = pltpu.get_barrier_semaphore()
     span = nx // 2 if nx % 2 == 0 else nx
@@ -100,9 +99,10 @@
 
     rows_out = [
         send(
-            row_send.at[s], row_recv.at[1 - s], row_ssem.at[s], row_rsem.at[1 - s], (sides[s], gy)
+            row_send.at[s, z], row_recv.at[1 - s, z], row_ssem.at[s, z], row_rsem.at[1 - s, z],
+            (sides[s], gy),
         )
-        for s in range(2)
+        for s in range(2) for z in range(ZOUT)
     ]
     corners_out = [
         send(
@@ -149,24 +149,26 @@
     ends_row, ends_lane = iota((16, lanes), 0), iota((16, lanes), 1)
     ends = [
         jnp.where(
-            (ends_row // 2 == 1 - e) & (ends_lane == ends_row % 2 + e * (lanes - 2)), 1.0, 0.0
+            (ends_row < 2) & (ends_lane == ends_row + e * (lanes - 2)), 1.0, 0.0
         ).astype(BF16)
         for e in range(2)
     ]
     for side in (1, 0):
-        for p in range(ZIN):
-            if side == 1:
-                for b in range(blocks):
-                    loads[p * blocks + b].wait()
-            for h in range(2):
-                part = [
-                    field[p, b, pl.ds(h * half, half)].reshape(half * SUB, lanes)
-                    for b in range(blocks if side == 1 else 1)
-                ]
-                found = dot(pick_rim[side], jnp.concatenate(part, axis=0) if side == 1 else part[0])
-                for r in range(2):
-                    rim[side, p, r, pl.ds(h * half, half), :] = found[r * half : (r + 1) * half]
         for z in range(ZOUT):
+            for p in planes[z]:
+                if side == 1:
+                    for b in range(blocks):
+                        loads[p, b].wait()
+                for h in range(2):
+                    part = [
+                        field[p, b, pl.ds(h * half, half)].reshape(half * SUB, lanes)
+                        for b in range(blocks if side == 1 else 1)
+                    ]
+                    found = dot(
+                        pick_rim[side], jnp.concatenate(part, axis=0) if side == 1 else part[0]
+                    )
+                    for r in range(2):
+                        rim[side, p, r, pl.ds(h * half, half), :] = found[r * half : (r + 1) * half]
             for r in range(2):
                 sums = [None, None, None]
                 for dz in (-1, 0, 1):
@@ -177,30 +179,29 @@
                 total = sums[1]
                 total = total + jnp.where(lane < lanes - 2, pltpu.roll(sums[2], lanes - 2, 1), 0.0)
                 total = total + jnp.where(lane >= 2, pltpu.roll(sums[0], 2, 1), 0.0)
-                row_send[side, pl.ds(r * C, C), pl.ds(z * lanes, lanes)] = total.astype(BF16)
+                row_send[side, z, pl.ds(r * C, C), :] = total.astype(BF16)
                 at = pl.ds(z * 2 * C + r * C, C)
                 rim_edge[side, 0, at, :] = sums[2].astype(BF16)
                 rim_edge[side, 1, at, :] = sums[0].astype(BF16)
-        if side == 1:
-            pl.semaphore_wait(barrier, jnp.where(first, ny - 1 + 3, ny - 1 + 6))
-            rows_out[1].start()
-
-            @pl.when(lax.rem(gx, span) == span - 1)
-            def _():
-                for y in (gy,) + lefts:
-                    pl.semaphore_signal(here, inc=1, device_id=(sides[1], y), device_id_type=MESH)
-
+            if side == 1 and z == 0:
+                pl.semaphore_wait(barrier, jnp.where(first, ny - 1 + 3, ny - 1 + 6))
+            if side == 1:
+                rows_out[ZOUT + z].start()
+            if side == 1 and z == 0:
+                @pl.when(lax.rem(gx, span) == span - 1)
+                def _():
+                    for y in (gy,) + lefts:
+                        pl.semaphore_signal(here, inc=1, device_id=(sides[1], y), device_id_type=MESH)
 
         for e in range(2):
-            corn_send[side, e] = dot(ends[e], rim_edge[side, e], NT)[:SUB]
+            corn_send[side, e] = dot(ends[e], rim_edge[side, e], NT)[:2]
 
     for copy in corners_out[2:]:
         copy.start()
 
     @pl.when(jnp.logical_not(first))
     def _():
-        rows_out[0].start()
-        for copy in corners_out[:2]:
+        for copy in rows_out[:ZOUT] + corners_out[:2]:
             copy.start()
 
     for copy in coarse_out:
@@ -342,11 +343,9 @@
 
     lax.fori_loop(0, C // 2, ready, 0)
 
-    back_row, back_lane = iota((SUB, lanes), 0), iota((SUB, lanes), 1)
+    back_row, back_lane = iota((4, lanes), 0), iota((4, lanes), 1)
     back = jnp.where(
-        (back_row < 4)
-        & (back_lane == jnp.where(back_row < 2, back_row, back_row + lanes - 4)),
-        1.0, 0.0,
+        back_lane == jnp.where(back_row < 2, back_row, back_row + lanes - 4), 1.0, 0.0
     ).astype(BF16)
     ends_k, ends_l = iota((32, ZOUT * lanes), 0), iota((32, ZOUT * lanes), 1)
     spot = ends_l % lanes - (ends_k // 16) * (lanes - 2)
@@ -354,8 +353,7 @@
     @pl.when(first)
     def _():
         pl.semaphore_wait(here, 3)
-        rows_out[0].start()
-        for copy in corners_out[:2]:
+        for copy in rows_out[:ZOUT] + corners_out[:2]:
             copy.start()
 
     for copy in corners_out + cols_out:
@@ -363,14 +361,17 @@
     cols = jnp.concatenate([col_recv[0], col_recv[1]], axis=0).astype(BF16)
     mixed_cols = dot(full, cols, NT).astype(BF16)
     corners = [
-        dot((corn_recv[side, 0] + corn_recv[side, 1]).astype(BF16), back, TN) for side in range(2)
+        dot(
+            jnp.concatenate([corn_recv[side, 0], corn_recv[side, 1]], axis=0).astype(BF16), back, TN
+        )
+        for side in range(2)
     ]
     for copy in rows_out:
         copy.wait_recv()
     arrived = []
     for side in range(2):
         parts = [
-            row_recv[side, :, pl.ds(z * lanes, lanes)].astype(F32)
+            row_recv[side, z].astype(F32)
             + corners[side][2 * C * z : 2 * C * (z + 1)]
             for z in range(ZOUT)
         ]
@@ -380,13 +381,14 @@
         at_lane = (ends_k % 16) // 2 == (ends_l // lanes) * blocks + b
         pick = jnp.where(at_lane & (spot == ends_k % 2), 1.0, 0.0).astype(BF16)
         right = jnp.concatenate(arrived + [pick], axis=0)
-        row_id = iota((block, ZOUT * lanes), 0) % SUB + SUB * b
         v = dot(jnp.concatenate([near_w[b], mixed_cols], axis=1), right)
         v = v + mixed[b].reshape(block, ZOUT * lanes)
-        v = base[b].reshape(block, ZOUT * lanes) + jnp.where(v > 0, v, 0.2 * v)
-        v = jnp.where(row_id < width, v, 0.0).astype(BF16)
+        v = base[b].reshape(block, ZOUT * lanes) + jnp.maximum(v, 0.2 * v)
         for z in range(ZOUT):
-            result[z, b] = v[:, z * lanes : (z + 1) * lanes].reshape(C, SUB, lanes)
+            tile = v[:, z * lanes : (z + 1) * lanes].reshape(C, SUB, lanes)
+            if b > 0:
+                tile = jnp.where(iota((1, SUB, lanes), 1) + SUB * b < width, tile, 0.0)
+            result[z, b] = tile.astype(BF16)
             stores.append(
                 pltpu.make_async_copy(
                     result.at[z, b], out.at[z, :, pl.ds(SUB * b, SUB), :], out_sem.at[z, b]
@@ -435,17 +437,17 @@
             vmem((2, ZIN, (blocks + 2) * SUB, lanes), F32),
             vmem((2, 2, ZOUT * 2 * C, lanes), BF16),
             vmem((ZIN, blocks, SUB, block), F32),
-            vmem((2, 2 * C, both), BF16),
-            vmem((2, 2 * C, both), BF16),
-            vmem((2, 2, SUB, ZOUT * 2 * C), F32),
-            vmem((2, 2, SUB, ZOUT * 2 * C), F32),
+            vmem((2, ZOUT, 2 * C, lanes), BF16),
+            vmem((2, ZOUT, 2 * C, lanes), BF16),
+            vmem((2, 2, 2, ZOUT * 2 * C), F32),
+            vmem((2, 2, 2, ZOUT * 2 * C), F32),
             vmem((2, 16, block), F32),
             vmem((2, 16, block), F32),
             vmem((SUB, ncols), F32),
             vmem((ny, SUB, ncols), F32),
             dma((8,)),
             dma((ZIN, blocks)),
-            dma((2,)), dma((2,)), dma((2, 2)), dma((2, 2)), dma((2,)), dma((2,)),
+            dma((2, ZOUT)), dma((2, ZOUT)), dma((2, 2)), dma((2, 2)), dma((2,)), dma((2,)),
             dma((ny - 1,)), dma((ny - 1,)),
             dma((ZOUT, blocks)),
             pltpu.SemaphoreType.REGULAR,

time: 25 us -> 24.4 us (0.976)
  Pallas kernels: 24 us -> 23.4 us
    pallas_call x1, Pallas kernels: 24 us -> 23.4 us  [shards(): pl.pallas_call(functools.partial(block_kernel, nx, ny), out_shape=jax.Sha...]
where the time goes in v4:
time: 24.4 us; the launch traced here: 24.3 us
  Pallas kernels  23.4 us (96%)
  local copies, waits for them, and re-layouts  0.88 us (4%)
    pallas_call x1, Pallas kernels, shards(): pl.pallas_call(functools.partial(block_kernel, nx, ny), out_shape=jax.Sha...  23.4 us
    unnamed x1, local copies, waits for them, and re-layouts  0.88 us

profile of v4, /device:TPU:8, one launch (start us, length us, event | category | flops | bytes accessed | tf_op | source)
XLA Modules:
  0.0 24.3 jit_solution(8750731708225480128)
XLA Ops:
  0.0 23.4 %block.1 = bf16[2,64,24,128]{3,2,1,0:T(8,128)(2,1)S(1)} custom-call(s32[32]{0:T(128)} %widths_h.1, f32[27,64]{1,0:T(8,128)} %dw_h.1, f32[64]{0:T(128)} %dwb_h.1, bf16[64,64]{1,0:T(8,128)(2,1)} %pw_h.1, f32[64]{0:T(128)} %pwb_h.1, f32[3,64]{1,0:T(4,128)} %bitcast.1, f32[3,2,128]{2,1,0:T(2,128)} %coarse_h.1, bf16[6,64,24,128]{3,2,1,0:T(8,128)(2,1)} %feat.1), custom_call_target="tpu_custom_call" | custom-call | tf_op jit(solution)/shard_map/block/pallas_call | solution.py:415
  23.4 0.9 %copy.10 = bf16[2,64,24,128]{3,2,1,0:T(8,128)(2,1)} copy(bf16[2,64,24,128]{3,2,1,0:T(8,128)(2,1)S(1)} %block.1) | data formatting | bytes 1572864

commit v5 on v4

--- a/solution.py
+++ b/solution.py
@@ -127,13 +127,16 @@
 
     eye = (iota((C, C), 0) == iota((C, C), 1)).astype(F32)
     by_channel = dot(eye, dw_v[...], NT, HIGH)
-    for side, dx in ((1, -1), (0, 1)):
+
+    def widen(side, dx):
         for dz in (-1, 0, 1):
             for dy in (-1, 0, 1):
                 t = tap(dz, dx, dy)
                 wide[side, 3 * (dz + 1) + dy + 1] = jnp.broadcast_to(
                     by_channel[:, t : t + 1], (C, lanes)
                 )
+
+    widen(1, -1)
 
     half = C // 2
     pick_row = iota((2 * half, half * SUB), 0)
@@ -154,6 +157,8 @@
         for e in range(2)
     ]
     for side in (1, 0):
+        if side == 0:
+            widen(0, 1)
         for z in range(ZOUT):
             for p in planes[z]:
                 if side == 1:

time: 24.4 us -> 24.4 us (level)
  no operation moved by 1% of the time
where the time goes in v5:
time: 24.4 us; the launch traced here: 24.2 us
  Pallas kernels  23.3 us (95%)
  local copies, waits for them, and re-layouts  0.88 us (4%)
    pallas_call x1, Pallas kernels, shards(): pl.pallas_call(functools.partial(block_kernel, nx, ny), out_shape=jax.Sha...  23.3 us
    unnamed x1, local copies, waits for them, and re-layouts  0.88 us

profile of v5, /device:TPU:8, one launch (start us, length us, event | category | flops | bytes accessed | tf_op | source)
XLA Modules:
  0.0 24.2 jit_solution(5788926133612006190)
XLA Ops:
  0.0 23.3 %block.1 = bf16[2,64,24,128]{3,2,1,0:T(8,128)(2,1)S(1)} custom-call(s32[32]{0:T(128)} %widths_h.1, f32[27,64]{1,0:T(8,128)} %dw_h.1, f32[64]{0:T(128)} %dwb_h.1, bf16[64,64]{1,0:T(8,128)(2,1)} %pw_h.1, f32[64]{0:T(128)} %pwb_h.1, f32[3,64]{1,0:T(4,128)} %bitcast.1, f32[3,2,128]{2,1,0:T(2,128)} %coarse_h.1, bf16[6,64,24,128]{3,2,1,0:T(8,128)(2,1)} %feat.1), custom_call_target="tpu_custom_call" | custom-call | tf_op jit(solution)/shard_map/block/pallas_call | solution.py:420
  23.3 0.9 %copy.10 = bf16[2,64,24,128]{3,2,1,0:T(8,128)(2,1)} copy(bf16[2,64,24,128]{3,2,1,0:T(8,128)(2,1)S(1)} %block.1) | data formatting | bytes 1572864
